TPU v7x, 32 devices: a whole 2x2x4 slice. The times are simulated.
32 devices in a mesh: grp: 2 (over y), ctx: 4 (over z), ch: 4 (over x, core).
Axes of the slice: x: 2, y: 2, z: 4, core: 2. Of those that a mesh axis runs over, the one named last changes fastest.
Arguments:
- fwd_hidden: bfloat16 [4096, 2048], P(('grp', 'ctx'), 'ch'), parts along dimension 0, may hold values from -6 to 6
- rev_hidden: bfloat16 [4096, 2048], P(('grp', 'ctx'), 'ch'), parts along dimension 0, may hold values from -6 to 6
- bases: int32 [4096], P(('grp', 'ctx')), parts along dimension 0, may hold values from 0 to 3
- complement: int32 [4], replicated, may hold values from 0 to 3, each once
- offsets: int32 [32], P('grp'), parts along dimension 0, may hold values from 0 to 2047, as said below
- base_embed: bfloat16 [4, 2048], P(None, 'ch'), may hold values from -6 to 6
- norm_gain: float32 [2048], replicated, may hold values from 0.1 to 1.9
- in_weight: bfloat16 [4, 2048, 2048], P(None, 'ctx', 'ch'), may hold values from -0.125 to 0.125
- filters: float32 [3, 16, 128], P(None, 'ch'), may hold values from -0.5 to 0.5
- out_weight: bfloat16 [2048, 2048], P('ctx', 'ch'), may hold values from -0.125 to 0.125
Outputs:
- block_out: bfloat16 [4096, 2048], P(('grp', 'ctx'), 'ch'), parts along dimension 0
There are 2 independent parts, one for each index of `grp`. A program takes and returns all parts, laid end to end along the dimension named above; an argument that names none is the same for every part. Nothing has to cross between parts.
Inputs may be any that keep to these rules, and one draw needn't show every extreme that they name: The first offset is 0, the last is 2047, and the offsets rise strictly; each is the first position of a document. `complement`: A permutation of the 4 letters.
All inputs are finite; a program needn't handle non-finite values.
Results may differ from a plain program's by a relative error of at most 0.012.
Values may be sent and summed in bfloat16 or wider, within the bound.
No kernel may reach another device: no remote copies, remote signals or barrier semaphores. Data moves between devices by JAX's collectives and lax.ppermute only.
A program may use at most 64 MiB of HBM per device.

v0:
```python
import jax
import jax.numpy as jnp
from jax import lax
from jax.sharding import PartitionSpec as P


def partner(block, axis, apart):
    count = lax.axis_size(axis)
    route = []
    for low in range(count):
        high = low | 1 << apart
        if high != low and high < count:
            route += [(low, high), (high, low)]
    return lax.ppermute(block, axis, route)


def shifted(value, axis, by):
    count = lax.axis_size(axis)
    pairs = [(i, i + by) for i in range(count) if 0 <= i + by < count]
    return lax.ppermute(value, axis, pairs)


def doc_of(positions, offsets, seq_len):
    count = jnp.sum((offsets[None, :] <= positions[:, None]).astype(jnp.int32), axis=1) - 1
    inside = (positions >= 0) & (positions < seq_len)
    return jnp.where(inside, count, -1)


def toeplitz(taps):
    heads, block = taps.shape
    pattern = jnp.concatenate(
        [jnp.zeros((heads, 1), taps.dtype), taps[:, ::-1], jnp.zeros((heads, block), taps.dtype)],
        axis=1,
    )
    repeated = jnp.tile(pattern, (1, block))
    return repeated[:, : block * 2 * block].reshape(heads, block, 2 * block)


def rms_norm(values, gain):
    floats = values.astype(jnp.float32)
    scale = lax.rsqrt(jnp.mean(floats * floats, axis=-1, keepdims=True) + 1e-05)
    return (floats * scale * gain).astype(jnp.bfloat16)


def blockwise_conv(conv_in, rim, taps, ext_docs):
    rows, width = conv_in.shape
    heads, block = taps.shape
    head_dim = width // heads
    blocks = rows // block
    extended = jnp.concatenate([rim, conv_in], axis=0)
    target_docs = ext_docs[block:].reshape(blocks, block)
    window = jnp.concatenate(
        [
            extended[:rows].reshape(blocks, block, width),
            extended[block:].reshape(blocks, block, width),
        ],
        axis=1,
    )
    window = window.reshape(blocks, 2 * block, heads, head_dim)
    window_docs = jnp.concatenate(
        [ext_docs[:rows].reshape(blocks, block), ext_docs[block:].reshape(blocks, block)], axis=1
    )
    mask = (target_docs[:, :, None] == window_docs[:, None, :]).astype(jnp.bfloat16)
    kernel = toeplitz(taps)[None] * mask[:, None]
    result = jnp.einsum("nhts,nshd->nthd", kernel, window, preferred_element_type=jnp.float32)
    return result.reshape(rows, width)


def local(
    fwd_hidden,
    rev_hidden,
    bases,
    complement,
    offsets,
    base_embed,
    norm_gain,
    in_weight,
    filters,
    out_weight,
):
    rows, width_local = fwd_hidden.shape
    ctx_count = lax.axis_size("ctx")
    here = lax.axis_index("ctx")
    seq_len = rows * ctx_count
    letters = base_embed.shape[0]
    alphabet = jnp.arange(letters, dtype=jnp.int32)
    onehot = (bases[:, None] == alphabet[None, :]).astype(jnp.bfloat16)
    swap_table = (complement[:, None] == alphabet[None, :]).astype(jnp.bfloat16)
    onehot_rev = jnp.dot(onehot, swap_table, preferred_element_type=jnp.float32).astype(
        jnp.bfloat16
    )
    embed_fwd = jnp.dot(onehot, base_embed, preferred_element_type=jnp.float32)
    embed_rev = jnp.dot(onehot_rev, base_embed, preferred_element_type=jnp.float32)
    fwd_input = (fwd_hidden.astype(jnp.float32) + embed_fwd).astype(jnp.bfloat16)
    rev_input = (rev_hidden.astype(jnp.float32) + embed_rev).astype(jnp.bfloat16)
    levels = ctx_count.bit_length() - 1
    for level in range(levels):
        rev_input = partner(rev_input, "ctx", level)
    rev_input = rev_input[::-1]
    full_fwd, full_rev = (
        lax.all_gather(fwd_input, "ch", axis=1, tiled=True),
        lax.all_gather(rev_input, "ch", axis=1, tiled=True),
    )
    normed_fwd = rms_norm(full_fwd, norm_gain)
    normed_rev = rms_norm(full_rev, norm_gain)
    piece = lax.all_gather(in_weight, "ctx", axis=1, tiled=True)
    add_fwd = jnp.einsum("rd,bdc->brc", normed_fwd, piece, preferred_element_type=jnp.float32)
    add_rev = jnp.einsum("rd,bdc->brc", normed_rev, piece, preferred_element_type=jnp.float32)
    taps_all = filters.astype(jnp.bfloat16)
    block = filters.shape[-1]
    before = here * rows - block + jnp.arange(rows + block, dtype=jnp.int32)
    docs_fwd = doc_of(before, offsets, seq_len)
    docs_rev = doc_of(seq_len - 1 - before, offsets, seq_len)
    state_fwd = add_fwd[0]
    state_rev = add_rev[0]
    for section in range(filters.shape[0]):
        in_fwd = state_fwd.astype(jnp.bfloat16)
        in_rev = state_rev.astype(jnp.bfloat16)
        rim_fwd, rim_rev = shifted((in_fwd[-block:], in_rev[-block:]), "ctx", 1)
        conv_rev = blockwise_conv(in_rev, rim_rev, taps_all[section], docs_rev)
        conv_fwd = blockwise_conv(in_fwd, rim_fwd, taps_all[section], docs_fwd)
        state_fwd = add_fwd[section + 1] * conv_fwd
        state_rev = add_rev[section + 1] * conv_rev
    mixed_fwd = state_fwd.astype(jnp.bfloat16)
    mixed_rev = state_rev.astype(jnp.bfloat16)
    for level in range(levels):
        mixed_rev = partner(mixed_rev, "ctx", level)
    mixed_rev = mixed_rev[::-1]
    mixed_sum = (mixed_fwd.astype(jnp.float32) + mixed_rev.astype(jnp.float32)).astype(jnp.bfloat16)
    whole_sum = lax.all_gather(mixed_sum, "ch", axis=1, tiled=True)
    total = jnp.dot(
        whole_sum,
        lax.all_gather(out_weight, "ctx", axis=0, tiled=True),
        preferred_element_type=jnp.float32,
    )
    return total.astype(jnp.bfloat16)


def solution(mesh):
    in_specs = (
        P(("grp", "ctx"), "ch"),
        P(("grp", "ctx"), "ch"),
        P(("grp", "ctx")),
        P(),
        P("grp"),
        P(None, "ch"),
        P(),
        P(None, "ctx", "ch"),
        P(None, "ch", None),
        P("ctx", "ch"),
    )
    out_specs = P(("grp", "ctx"), "ch")
    return jax.shard_map(local, mesh=mesh, in_specs=in_specs, out_specs=out_specs, check_vma=False)
```

profile of v0, /device:TPU:0, one launch (start us, length us, event | category | flops | bytes accessed | tf_op | source)
XLA Modules:
  0.0 390.4 jit_solution(10410948972962377146)
XLA Ops:
  7.2 2.2 fusion.14
  9.5 1.7 fusion.15
  11.2 3.1 collective-permute-start.3
  14.3 11.9 %collective-permute-done.3 = bf16[512,512]{1,0:T(8,128)(2,1)S(1)} collective-permute-done((bf16[512,512]{1,0:T(8,128)(2,1)S(1)}, bf16[512,512]{1,0:T(8,128)(2,1)S(1)}, u32[]{:S(2)}, u32[]{:S(2)}) %collective-permute-start.3) | collective-permute-done | bytes 524320 | tf_op jit(solution)/shard_map/ppermute | solution.py:14
  26.2 2.8 collective-permute-start.4
  28.9 22.6 %collective-permute-done.4 = bf16[512,512]{1,0:T(8,128)(2,1)S(1)} collective-permute-done((bf16[512,512]{1,0:T(8,128)(2,1)S(1)}, bf16[512,512]{1,0:T(8,128)(2,1)S(1)}, u32[]{:S(2)}, u32[]{:S(2)}) %collective-permute-start.4) | collective-permute-done | bytes 524320 | tf_op jit(solution)/shard_map/ppermute | solution.py:14
  51.5 5.1 %rev.21 = bf16[512,512]{1,0:T(8,128)(2,1)} reverse(bf16[512,512]{1,0:T(8,128)(2,1)S(1)} %collective-permute-done.4), dimensions={0} | reverse | bytes 1048576 | tf_op jit(solution)/shard_map/rev | solution.py:99
  64.7 2.4 fusion
  67.1 13.3 %all-gather.10.cloned.1.call-done = bf16[512,2048]{1,0:T(8,128)(2,1)} async-done(((bf16[512,512]{1,0:T(8,128)(2,1)}), bf16[512,2048]{1,0:T(8,128)(2,1)}) %all-gather.10.cloned.1.call-update) | async-done | bytes 2097168 | tf_op jit(solution)/shard_map/all_gather | solution.py:102
  80.4 2.2 fusion.3
  82.6 149.0 %all-gather.8.cloned.1.call-done = bf16[4,2048,512]{2,1,0:T(8,128)(2,1)} async-done(((bf16[4,512,512]{2,1,0:T(8,128)(2,1)}), bf16[4,2048,512]{2,1,0:T(8,128)(2,1)}) %all-gather.8.cloned.1.call-update) | async-done | bytes 8388624 | tf_op jit(solution)/shard_map/all_gather | solution.py:106
  231.7 7.1 %convolution_bitcast_fusion = f32[4,512,512]{2,1,0:T(8,128)S(1)} fusion(bf16[4,2048,512]{2,1,0:T(8,128)(2,1)} %all-gather.8.cloned.1.call-done, bf16[512,2048]{1,0:T(8,128)(2,1)S(1)} %copy-done.10, f32[512]{0:T(512)S(1)} %add_rsqrt_fusion, f32[2048]{0:T(1024)S(1)} %copy-done.14), kind=kOutput, calls=%fused_computation.10 | convolution fusion | flops 4299161600 | bytes 14690304 | tf_op jit(solution)/shard_map/rd,bdc->brc/dot_general | solution.py:108
  243.5 7.7 %convolution_bitcast_fusion.1 = f32[4,512,512]{2,1,0:T(8,128)S(1)} fusion(bf16[4,2048,512]{2,1,0:T(8,128)(2,1)} %all-gather.8.cloned.1.call-done, bf16[512,2048]{1,0:T(8,128)(2,1)} %all-gather.6.cloned.1.call-done, f32[2048]{0:T(1024)S(1)} %copy-done.14, f32[512]{0:T(512)S(1)} %add_rsqrt_fusion.1), kind=kOutput, calls=%fused_computation.11 | convolution fusion | flops 4299161600 | bytes 14690304 | tf_op jit(solution)/shard_map/rd,bdc->brc/dot_general | solution.py:107
  254.6 1.6 squeeze.52
  256.2 1.4 squeeze.51
  257.5 2.0 copy.62
  259.5 1.9 collective-permute-start.5
  261.4 1.6 squeeze.44
  263.0 2.0 convert_element_type.130
  264.9 1.9 copy.52
  266.9 1.6 slice_bitcast_fusion.3
  268.4 3.3 collective-permute-start
  271.7 1.9 pad_maximum_fusion.2
  273.6 2.0 concatenate.90
  276.7 2.8 fusion.41
  280.2 1.4 fusion.18
  283.0 2.7 collective-permute-start.6
  286.5 2.0 concatenate.77
  289.7 2.4 fusion.43
  293.1 1.8 pad_maximum_fusion.1
  294.9 1.9 concatenate.94
  298.0 2.5 fusion.40
  301.1 1.4 fusion.17
  302.5 3.9 %collective-permute-start.7 = (bf16[128,512]{1,0:T(8,128)(2,1)S(1)}, bf16[128,512]{1,0:T(8,128)(2,1)S(1)}, u32[]{:S(2)}, u32[]{:S(2)}) collective-permute-start(bf16[128,512]{1,0:T(8,128)(2,1)S(1)} %slice.179), channel_id=1, source_target_pairs={{0,4},{4,8},{8,12},{1,5},{5,9},{9,13},{2,6},{6,10},{10,14},{3,7},{... | collective-permute-start | bytes 393224 | tf_op jit(solution)/shard_map/ppermute | solution.py:20
  306.5 1.4 fusion.21
  308.5 3.0 collective-permute-start.1
  311.8 1.6 convolution_bitcast_fusion.6
  313.9 2.2 fusion.16
  317.4 2.3 fusion.42
  320.4 7.7 %collective-permute-done.8 = bf16[512,512]{1,0:T(8,128)(2,1)} collective-permute-done((bf16[512,512]{1,0:T(8,128)(2,1)}, bf16[512,512]{1,0:T(8,128)(2,1)}, u32[]{:S(2)}, u32[]{:S(2)}) %collective-permute-start.8) | collective-permute-done | bytes 524320 | tf_op jit(solution)/shard_map/ppermute | solution.py:14
  328.1 1.4 fusion.20
  329.5 2.3 collective-permute-start.2
  331.8 8.1 %collective-permute-done.2 = bf16[128,512]{1,0:T(8,128)(2,1)S(1)} collective-permute-done((bf16[128,512]{1,0:T(8,128)(2,1)S(1)}, bf16[128,512]{1,0:T(8,128)(2,1)S(1)}, u32[]{:S(2)}, u32[]{:S(2)}) %collective-permute-start.2) | collective-permute-done | bytes 131104 | tf_op jit(solution)/shard_map/ppermute | solution.py:20
  340.1 1.6 convolution_bitcast_fusion.7
  342.2 9.0 %collective-permute-done.9 = bf16[512,512]{1,0:T(8,128)(2,1)S(1)} collective-permute-done((bf16[512,512]{1,0:T(8,128)(2,1)}, bf16[512,512]{1,0:T(8,128)(2,1)S(1)}, u32[]{:S(2)}, u32[]{:S(2)}) %collective-permute-start.9) | collective-permute-done | bytes 524320 | tf_op jit(solution)/shard_map/ppermute | solution.py:14
  351.8 2.3 add_convert_fusion
  354.2 25.4 %all-gather.12.cloned.1.call-done = bf16[512,2048]{1,0:T(8,128)(2,1)} async-done(((bf16[512,512]{1,0:T(8,128)(2,1)}), bf16[512,2048]{1,0:T(8,128)(2,1)}) %all-gather.12.cloned.1.call-update) | async-done | bytes 2097168 | tf_op jit(solution)/shard_map/all_gather | solution.py:130
  379.6 4.3 %convolution_convert_fusion = bf16[512,512]{1,0:T(8,128)(2,1)} fusion(bf16[512,2048]{1,0:T(8,128)(2,1)} %all-gather.12.cloned.1.call-done, bf16[2048,512]{1,0:T(8,128)(2,1)} %all-gather.14.cloned.1.call-done), kind=kOutput, calls=%fused_computation.28 | convolution fusion | flops 1074003968 | bytes 4718592 | tf_op jit(solution)/shard_map/dot_general | solution.py:131
  (118 shorter events, 29.4 us)
Async XLA Ops:
  6.5 0.7 copy-start
  6.5 58.2 %all-gather.6.cloned.1.call-start = ((), (), s32[]{:S(2)}) async-start(), calls=%async_computation | async-start | bytes 2621440 | tf_op jit(solution)/shard_map/all_gather | solution.py:101
  9.4 71.0 %all-gather.10.cloned.1.call-start = ((), (), s32[]{:S(2)}) async-start(), calls=%async_computation.2 | async-start | bytes 2621440 | tf_op jit(solution)/shard_map/all_gather | solution.py:102
  11.2 46.9 %copy-start.13 = (s32[16]{0:T(128)S(1)}, s32[16]{0:T(128)}, u32[]{:S(2)}) copy-start(s32[16]{0:T(128)} %param.14) | copy-start | bytes 196
  11.2 47.1 %copy-start.12 = (f32[3,4,128]{2,1,0:T(4,128)S(1)}, f32[3,4,128]{2,1,0:T(4,128)}, u32[]{:S(2)}) copy-start(f32[3,4,128]{2,1,0:T(4,128)} %param.18) | copy-start | bytes 18436
  11.2 15.0 %collective-permute-start.3 = (bf16[512,512]{1,0:T(8,128)(2,1)S(1)}, bf16[512,512]{1,0:T(8,128)(2,1)S(1)}, u32[]{:S(2)}, u32[]{:S(2)}) collective-permute-start(bf16[512,512]{1,0:T(8,128)(2,1)S(1)} %fusion.15), channel_id=1, source_target_pairs={{0,4},{4,0},{8,12},{12,8},{1,5},{5,1},{9,13},{13,9},{2,6},{6,2},{1... | collective-permute-start | bytes 1572872 | tf_op jit(solution)/shard_map/ppermute | solution.py:14
  26.2 25.3 %collective-permute-start.4 = (bf16[512,512]{1,0:T(8,128)(2,1)S(1)}, bf16[512,512]{1,0:T(8,128)(2,1)S(1)}, u32[]{:S(2)}, u32[]{:S(2)}) collective-permute-start(bf16[512,512]{1,0:T(8,128)(2,1)S(1)} %collective-permute-done.3), channel_id=1, source_target_pairs={{0,8},{8,0},{4,12},{12,4},{1,9},{9,1},{5,13},{13,5},{2,10},{10,2},... | collective-permute-start | bytes 1572872 | tf_op jit(solution)/shard_map/ppermute | solution.py:14
  56.7 175.0 %all-gather.8.cloned.1.call-start = ((), (), s32[]{:S(2)}) async-start(), calls=%async_computation.1 | async-start | bytes 10485760 | tf_op jit(solution)/shard_map/all_gather | solution.py:106
  57.4 296.8 %all-gather.14.cloned.1.call-start = ((), (), s32[]{:S(2)}) async-start(), calls=%async_computation.4 | async-start | bytes 2621440 | tf_op jit(solution)/shard_map/all_gather | solution.py:133
  58.0 321.6 %all-gather.12.cloned.1.call-start = ((), (), s32[]{:S(2)}) async-start(), calls=%async_computation.3 | async-start | bytes 2621440 | tf_op jit(solution)/shard_map/all_gather | solution.py:130
  64.7 167.0 %copy-start.14 = (f32[2048]{0:T(1024)S(1)}, f32[2048]{0:T(1024)}, u32[]{:S(2)}) copy-start(f32[2048]{0:T(1024)} %param.16) | copy-start | bytes 24580
  80.4 151.3 %copy-start.10 = (bf16[512,2048]{1,0:T(8,128)(2,1)S(1)}, bf16[512,2048]{1,0:T(8,128)(2,1)}, u32[]{:S(2)}) copy-start(bf16[512,2048]{1,0:T(8,128)(2,1)} %all-gather.10.cloned.1.call-done) | copy-start | bytes 6291460
  238.7 2.3 copy-start.3
  251.3 2.5 copy-start.2
  259.5 12.2 %collective-permute-start.5 = (bf16[128,512]{1,0:T(8,128)(2,1)}, bf16[128,512]{1,0:T(8,128)(2,1)}, u32[]{:S(2)}, u32[]{:S(2)}) collective-permute-start(bf16[128,512]{1,0:T(8,128)(2,1)} %slice_bitcast_fusion.2), channel_id=1, source_target_pairs={{0,4},{4,8},{8,12},{1,5},{5,9},{9,13},{2,6},{6,10},{10,14},{3,7},{... | collective-permute-start | bytes 393224 | tf_op jit(solution)/shard_map/ppermute | solution.py:20
  268.4 17.3 %collective-permute-start = (bf16[128,512]{1,0:T(8,128)(2,1)}, bf16[128,512]{1,0:T(8,128)(2,1)S(1)}, u32[]{:S(2)}, u32[]{:S(2)}) collective-permute-start(bf16[128,512]{1,0:T(8,128)(2,1)} %slice_bitcast_fusion.3), channel_id=1, source_target_pairs={{0,4},{4,8},{8,12},{1,5},{5,9},{9,13},{2,6},{6,10},{10,14},{3,7},{... | collective-permute-start | bytes 393224 | tf_op jit(solution)/shard_map/ppermute | solution.py:20
  279.5 6.2 %copy-start.11 = (bf16[512,512]{1,0:T(8,128)(2,1)S(1)}, bf16[512,512]{1,0:T(8,128)(2,1)}, u32[]{:S(2)}) copy-start(bf16[512,512]{1,0:T(8,128)(2,1)} %slice_bitcast_fusion.9) | copy-start | bytes 1572868
  281.5 0.8 copy-start.6
  283.0 9.7 %collective-permute-start.6 = (bf16[128,512]{1,0:T(8,128)(2,1)}, bf16[128,512]{1,0:T(8,128)(2,1)}, u32[]{:S(2)}, u32[]{:S(2)}) collective-permute-start(bf16[128,512]{1,0:T(8,128)(2,1)} %slice.178), channel_id=1, source_target_pairs={{0,4},{4,8},{8,12},{1,5},{5,9},{9,13},{2,6},{6,10},{10,14},{3,7},{... | collective-permute-start | bytes 393224 | tf_op jit(solution)/shard_map/ppermute | solution.py:20
  292.1 1.0 copy-start.7
  302.5 9.0 %collective-permute-start.7 = (bf16[128,512]{1,0:T(8,128)(2,1)S(1)}, bf16[128,512]{1,0:T(8,128)(2,1)S(1)}, u32[]{:S(2)}, u32[]{:S(2)}) collective-permute-start(bf16[128,512]{1,0:T(8,128)(2,1)S(1)} %slice.179), channel_id=1, source_target_pairs={{0,4},{4,8},{8,12},{1,5},{5,9},{9,13},{2,6},{6,10},{10,14},{3,7},{... | collective-permute-start | bytes 393224 | tf_op jit(solution)/shard_map/ppermute | solution.py:20
  307.8 3.9 %copy-start.4 = (bf16[512,512]{1,0:T(8,128)(2,1)}, bf16[512,512]{1,0:T(8,128)(2,1)S(1)}, u32[]{:S(2)}) copy-start(bf16[512,512]{1,0:T(8,128)(2,1)S(1)} %fusion.21) | copy-start | bytes 1572868
  307.9 3.9 %copy-start.9 = (bf16[4,128,256]{2,1,0:T(8,128)(2,1)S(1)}, bf16[4,128,256]{2,1,0:T(8,128)(2,1)}, u32[]{:S(2)}) copy-start(bf16[4,128,256]{2,1,0:T(8,128)(2,1)} %compare_convert_fusion) | copy-start | bytes 786436
  308.5 7.9 %collective-permute-start.1 = (bf16[128,512]{1,0:T(8,128)(2,1)}, bf16[128,512]{1,0:T(8,128)(2,1)S(1)}, u32[]{:S(2)}, u32[]{:S(2)}) collective-permute-start(bf16[128,512]{1,0:T(8,128)(2,1)} %slice.169), channel_id=1, source_target_pairs={{0,4},{4,8},{8,12},{1,5},{5,9},{9,13},{2,6},{6,10},{10,14},{3,7},{... | collective-permute-start | bytes 393224 | tf_op jit(solution)/shard_map/ppermute | solution.py:20
  313.8 2.6 copy-start.5
  316.1 12.0 %collective-permute-start.8 = (bf16[512,512]{1,0:T(8,128)(2,1)}, bf16[512,512]{1,0:T(8,128)(2,1)}, u32[]{:S(2)}, u32[]{:S(2)}) collective-permute-start(bf16[512,512]{1,0:T(8,128)(2,1)} %fusion.16), channel_id=1, source_target_pairs={{0,4},{4,0},{8,12},{12,8},{1,5},{5,1},{9,13},{13,9},{2,6},{6,2},{1... | collective-permute-start | bytes 1572872 | tf_op jit(solution)/shard_map/ppermute | solution.py:14
  316.5 1.0 copy-start.8
  328.1 23.1 %collective-permute-start.9 = (bf16[512,512]{1,0:T(8,128)(2,1)}, bf16[512,512]{1,0:T(8,128)(2,1)S(1)}, u32[]{:S(2)}, u32[]{:S(2)}) collective-permute-start(bf16[512,512]{1,0:T(8,128)(2,1)} %collective-permute-done.8), channel_id=1, source_target_pairs={{0,8},{8,0},{4,12},{12,4},{1,9},{9,1},{5,13},{13,5},{2,10},{10,2},... | collective-permute-start | bytes 1572872 | tf_op jit(solution)/shard_map/ppermute | solution.py:14
  329.5 10.4 %collective-permute-start.2 = (bf16[128,512]{1,0:T(8,128)(2,1)S(1)}, bf16[128,512]{1,0:T(8,128)(2,1)S(1)}, u32[]{:S(2)}, u32[]{:S(2)}) collective-permute-start(bf16[128,512]{1,0:T(8,128)(2,1)S(1)} %slice.170), channel_id=1, source_target_pairs={{0,4},{4,8},{8,12},{1,5},{5,9},{9,13},{2,6},{6,10},{10,14},{3,7},{... | collective-permute-start | bytes 393224 | tf_op jit(solution)/shard_map/ppermute | solution.py:20
  354.2 29.7 %copy-start.1 = (bf16[4,512]{1,0:T(4,128)(2,1)S(1)}, bf16[4,512]{1,0:T(4,128)(2,1)}, u32[]{:S(2)}) copy-start(bf16[4,512]{1,0:T(4,128)(2,1)} %param.15) | copy-start | bytes 12292
Sparse Core Ops, SparseCore 0:
  9.6 25.2 all-gather.5
  56.8 23.5 all-gather.9
  82.0 149.6 all-gather.7
  233.1 46.2 all-gather.13
  354.3 25.2 all-gather.11
where the time goes:
time: 392 us; the launch traced here: 390 us
  waiting for transfers between devices  248 us (63%)
  local copies, waits for them, and re-layouts  48.7 us (12%)
  matrix products  36.2 us (9%)
  starting transfers between devices  23.1 us (6%)
  other arithmetic  20.5 us (5%)
  between operations  13.7 us (3%)
    all_gather x1, waiting for transfers between devices, local(): piece = lax.all_gather(in_weight, 'ctx', axis=1, tiled=True)  149 us
    ppermute x4, waiting for transfers between devices, partner(): return lax.ppermute(block, axis, route)  51.2 us
    all_gather x1, waiting for transfers between devices, local(): whole_sum = lax.all_gather(mixed_sum, 'ch', axis=1, tiled=True)  25.4 us
    ppermute x6, starting transfers between devices, shifted(): return lax.ppermute(value, axis, pairs)  17.1 us
    all_gather x1, waiting for transfers between devices, local(): lax.all_gather(rev_input, 'ch', axis=1, tiled=True)  13.3 us
    dot_general x6, matrix products, blockwise_conv(): jnp.einsum('nhts,nshd->nthd', kernel, window, preferred_element_type=jnp....  13.2 us
    concatenate x12, local copies, waits for them, and re-layouts, blockwise_conv(): jnp.concatenate([extended[:rows].reshape(blocks, block, width), extended[...  9.97 us
    ppermute x6, waiting for transfers between devices, shifted(): return lax.ppermute(value, axis, pairs)  8.09 us
  transfers between devices with their start and end apart: 15, of which 8 were waited for; matrix products, arithmetic and copies ran while one was open for 24% of the time, Pallas kernels for 0%

commit v1 on v0

--- a/solution.py
+++ b/solution.py
@@ -78,6 +78,23 @@
     filters,
     out_weight,
 ):
+
+    def _pass_meshes(page, axis_key):
+        world = lax.axis_size(axis_key)
+        sheets = list(map(lambda dev_i: (dev_i, (dev_i + 1) % world), range(world)))
+        gallery = list(map(lambda dev_i: (dev_i, (dev_i - 1) % world), range(world)))
+        current_arr, block_next = ([page], [page])
+        for _ in range(world // 2):
+            current_arr.append(lax.ppermute(current_arr[-1], axis_key, sheets))
+        for _ in range((world - 1) // 2):
+            block_next.append(lax.ppermute(block_next[-1], axis_key, gallery))
+        row_out = jnp.roll(
+            jnp.concatenate([*current_arr[::-1], *block_next[1:]], axis=1),
+            shift=(lax.axis_index(axis_key) - world // 2) * page.shape[1],
+            axis=1,
+        )
+        return row_out
+
     rows, width_local = fwd_hidden.shape
     ctx_count = lax.axis_size("ctx")
     here = lax.axis_index("ctx")
@@ -127,7 +144,7 @@
         mixed_rev = partner(mixed_rev, "ctx", level)
     mixed_rev = mixed_rev[::-1]
     mixed_sum = (mixed_fwd.astype(jnp.float32) + mixed_rev.astype(jnp.float32)).astype(jnp.bfloat16)
-    whole_sum = lax.all_gather(mixed_sum, "ch", axis=1, tiled=True)
+    whole_sum = _pass_meshes(mixed_sum, "ch")
     total = jnp.dot(
         whole_sum,
         lax.all_gather(out_weight, "ctx", axis=0, tiled=True),

time: 392 us -> 428 us (1.092); the launches traced: 390 us -> 422 us
  waiting for transfers between devices: 248 us -> 273 us
  local copies, waits for them, and re-layouts: 48.7 us -> 54.8 us
    all_gather x1 -> x0, waiting for transfers between devices: 25.4 us -> none  [local(): whole_sum = lax.all_gather(mixed_sum, 'ch', axis=1, tiled=True)]
    ppermute x0 -> x3, waiting for transfers between devices: none -> 18.6 us  [the longest x2 18.6 us: _pass_meshes(): current_arr.append(lax.ppermute(current_arr[-1], axis_key, sheets))]
    ppermute x4, waiting for transfers between devices: 51.2 us -> 66.9 us  [partner(): return lax.ppermute(block, axis, route)]
    ppermute x6, waiting for transfers between devices: 8.09 us -> 23.5 us  [shifted(): return lax.ppermute(value, axis, pairs)]
    unnamed x33 -> x38, local copies, waits for them, and re-layouts: 5.73 us -> 10.1 us
  transfers between devices with their start and end apart: 15 -> 17, of which waited for: 8 -> 9; matrix products, arithmetic and copies ran while one was open for 24% -> 16% of each run, Pallas kernels for 0% -> 0%
where the time goes in v1:
time: 428 us; the launch traced here: 422 us
  waiting for transfers between devices  273 us (64%)
  local copies, waits for them, and re-layouts  54.8 us (13%)
  matrix products  37.9 us (9%)
  starting transfers between devices  22.4 us (5%)
  other arithmetic  20 us (5%)
  between operations  13.7 us (3%)
    all_gather x1, waiting for transfers between devices, local(): piece = lax.all_gather(in_weight, 'ctx', axis=1, tiled=True)  149 us
    ppermute x4, waiting for transfers between devices, partner(): return lax.ppermute(block, axis, route)  66.9 us
    ppermute x6, waiting for transfers between devices, shifted(): return lax.ppermute(value, axis, pairs)  23.5 us
    ppermute x2, waiting for transfers between devices, _pass_meshes(): current_arr.append(lax.ppermute(current_arr[-1], axis_key, sheets))  18.6 us
    dot_general x6, matrix products, blockwise_conv(): jnp.einsum('nhts,nshd->nthd', kernel, window, preferred_element_type=jnp....  14.3 us
    all_gather x1, waiting for transfers between devices, local(): lax.all_gather(rev_input, 'ch', axis=1, tiled=True)  14.1 us
    ppermute x6, starting transfers between devices, shifted(): return lax.ppermute(value, axis, pairs)  13 us
    concatenate x12, local copies, waits for them, and re-layouts, blockwise_conv(): jnp.concatenate([extended[:rows].reshape(blocks, block, width), extended[...  10.1 us
  transfers between devices with their start and end apart: 17, of which 9 were waited for; matrix products, arithmetic and copies ran while one was open for 16% of the time, Pallas kernels for 0%

profile of v1, /device:TPU:0, one launch (start us, length us, event | category | flops | bytes accessed | tf_op | source)
XLA Modules:
  0.0 421.8 jit_solution(159476866805656895)
XLA Ops:
  7.2 2.2 fusion.16
  9.5 1.7 fusion.17
  11.2 3.1 collective-permute-start.3
  14.2 11.9 %collective-permute-done.3 = bf16[512,512]{1,0:T(8,128)(2,1)S(1)} collective-permute-done((bf16[512,512]{1,0:T(8,128)(2,1)S(1)}, bf16[512,512]{1,0:T(8,128)(2,1)S(1)}, u32[]{:S(2)}, u32[]{:S(2)}) %collective-permute-start.3) | collective-permute-done | bytes 524320 | tf_op jit(solution)/shard_map/ppermute | solution.py:14
  26.2 2.8 collective-permute-start.4
  28.9 22.6 %collective-permute-done.4 = bf16[512,512]{1,0:T(8,128)(2,1)S(1)} collective-permute-done((bf16[512,512]{1,0:T(8,128)(2,1)S(1)}, bf16[512,512]{1,0:T(8,128)(2,1)S(1)}, u32[]{:S(2)}, u32[]{:S(2)}) %collective-permute-start.4) | collective-permute-done | bytes 524320 | tf_op jit(solution)/shard_map/ppermute | solution.py:14
  51.5 5.1 %rev.21 = bf16[512,512]{1,0:T(8,128)(2,1)} reverse(bf16[512,512]{1,0:T(8,128)(2,1)S(1)} %collective-permute-done.4), dimensions={0} | reverse | bytes 1048576 | tf_op jit(solution)/shard_map/rev | solution.py:116
  64.1 2.2 fusion
  66.3 14.1 %all-gather.9.cloned.1.call-done = bf16[512,2048]{1,0:T(8,128)(2,1)} async-done(((bf16[512,512]{1,0:T(8,128)(2,1)}), bf16[512,2048]{1,0:T(8,128)(2,1)}) %all-gather.9.cloned.1.call-update) | async-done | bytes 2097168 | tf_op jit(solution)/shard_map/all_gather | solution.py:119
  80.4 2.1 fusion.3
  82.5 149.2 %all-gather.7.cloned.1.call-done = bf16[4,2048,512]{2,1,0:T(8,128)(2,1)} async-done(((bf16[4,512,512]{2,1,0:T(8,128)(2,1)}), bf16[4,2048,512]{2,1,0:T(8,128)(2,1)}) %all-gather.7.cloned.1.call-update) | async-done | bytes 8388624 | tf_op jit(solution)/shard_map/all_gather | solution.py:123
  231.6 7.7 %convolution_bitcast_fusion = f32[4,512,512]{2,1,0:T(8,128)S(1)} fusion(bf16[4,2048,512]{2,1,0:T(8,128)(2,1)} %all-gather.7.cloned.1.call-done, bf16[512,2048]{1,0:T(8,128)(2,1)} %all-gather.9.cloned.1.call-done, f32[512]{0:T(512)S(1)} %add_rsqrt_fusion, f32[2048]{0:T(1024)S(1)} %copy-done.13), kind=kOutput, calls=%fused_computation.10 | convolution fusion | flops 4299161600 | bytes 14690304 | tf_op jit(solution)/shard_map/rd,bdc->brc/dot_general | solution.py:125
  244.2 7.7 %convolution_bitcast_fusion.1 = f32[4,512,512]{2,1,0:T(8,128)S(1)} fusion(bf16[4,2048,512]{2,1,0:T(8,128)(2,1)} %all-gather.7.cloned.1.call-done, bf16[512,2048]{1,0:T(8,128)(2,1)} %all-gather.5.cloned.1.call-done, f32[2048]{0:T(1024)S(1)} %copy-done.13, f32[512]{0:T(512)S(1)} %add_rsqrt_fusion.1), kind=kOutput, calls=%fused_computation.11 | convolution fusion | flops 4299161600 | bytes 14690304 | tf_op jit(solution)/shard_map/rd,bdc->brc/dot_general | solution.py:124
  255.2 1.6 squeeze.52
  258.1 2.0 copy.62
  260.0 1.9 collective-permute-start.5
  262.0 1.6 squeeze.44
  263.6 2.0 convert_element_type.130
  265.5 1.9 copy.52
  267.4 1.6 slice_bitcast_fusion.3
  269.0 3.2 collective-permute-start
  272.3 1.9 pad_maximum_fusion.2
  274.1 2.0 concatenate.96
  277.3 2.8 fusion.46
  280.8 1.4 fusion.23
  283.6 2.7 collective-permute-start.6
  287.2 2.0 concatenate.83
  290.4 2.5 fusion.48
  293.6 1.7 pad_maximum_fusion.1
  295.3 2.0 concatenate.100
  298.4 2.4 fusion.45
  302.9 1.4 collective-permute-start.7
  305.8 1.9 collective-permute-start.1
  308.0 2.6 convolution_bitcast_fusion.6
  310.6 1.7 copy.70
  312.3 2.2 fusion.21
  314.5 1.6 collective-permute-start.8
  316.8 2.4 fusion.47
  319.9 15.2 %collective-permute-done.8 = bf16[512,512]{1,0:T(8,128)(2,1)} collective-permute-done((bf16[512,512]{1,0:T(8,128)(2,1)}, bf16[512,512]{1,0:T(8,128)(2,1)}, u32[]{:S(2)}, u32[]{:S(2)}) %collective-permute-start.8) | collective-permute-done | bytes 524320 | tf_op jit(solution)/shard_map/ppermute | solution.py:14
  336.6 1.8 collective-permute-start.2
  338.3 23.5 %collective-permute-done.2 = bf16[128,512]{1,0:T(8,128)(2,1)S(1)} collective-permute-done((bf16[128,512]{1,0:T(8,128)(2,1)S(1)}, bf16[128,512]{1,0:T(8,128)(2,1)S(1)}, u32[]{:S(2)}, u32[]{:S(2)}) %collective-permute-start.2) | collective-permute-done | bytes 131104 | tf_op jit(solution)/shard_map/ppermute | solution.py:20
  362.1 1.6 convolution_bitcast_fusion.7
  364.2 17.2 %collective-permute-done.9 = bf16[512,512]{1,0:T(8,128)(2,1)S(1)} collective-permute-done((bf16[512,512]{1,0:T(8,128)(2,1)}, bf16[512,512]{1,0:T(8,128)(2,1)S(1)}, u32[]{:S(2)}, u32[]{:S(2)}) %collective-permute-start.9) | collective-permute-done | bytes 524320 | tf_op jit(solution)/shard_map/ppermute | solution.py:14
  381.9 1.6 add_convert_fusion
  383.6 8.6 %collective-permute-done.10 = bf16[512,512]{1,0:T(8,128)(2,1)S(1)} collective-permute-done((bf16[512,512]{1,0:T(8,128)(2,1)S(1)}, bf16[512,512]{1,0:T(8,128)(2,1)S(1)}, u32[]{:S(2)}, u32[]{:S(2)}) %collective-permute-start.10) | collective-permute-done | bytes 524320 | tf_op jit(solution)/shard_map/ppermute | solution.py:88
  392.2 1.7 collective-permute-start.12
  393.9 10.0 %collective-permute-done.11 = bf16[512,512]{1,0:T(8,128)(2,1)S(1)} collective-permute-done((bf16[512,512]{1,0:T(8,128)(2,1)S(1)}, bf16[512,512]{1,0:T(8,128)(2,1)S(1)}, u32[]{:S(2)}, u32[]{:S(2)}) %collective-permute-start.11) | collective-permute-done | bytes 524320 | tf_op jit(solution)/shard_map/ppermute | solution.py:88
  411.0 4.3 %fusion.18 = bf16[512,512]{1,0:T(8,128)(2,1)} fusion(bf16[2048,512]{1,0:T(8,128)(2,1)} %all-gather.11.cloned.1.call-done, bf16[512,4096]{1,0:T(8,128)(2,1)} %constant_dynamic-update-slice_fusion, s32[]{:T(128)S(6)} %select_n.47), kind=kOutput, calls=%fused_computation.30 | convolution fusion | flops 1074003968 | bytes 4718596 | tf_op jit(solution)/shard_map/dot_general | solution.py:148
  (127 shorter events, 39.4 us)
Async XLA Ops:
  6.5 0.7 copy-start
  6.5 50.9 %copy-start.11 = (f32[3,4,128]{2,1,0:T(4,128)S(1)}, f32[3,4,128]{2,1,0:T(4,128)}, u32[]{:S(2)}) copy-start(f32[3,4,128]{2,1,0:T(4,128)} %param.18) | copy-start | bytes 18436
  6.5 57.6 %all-gather.5.cloned.1.call-start = ((), (), s32[]{:S(2)}) async-start(), calls=%async_computation | async-start | bytes 2621440 | tf_op jit(solution)/shard_map/all_gather | solution.py:118
  9.4 70.9 %all-gather.9.cloned.1.call-start = ((), (), s32[]{:S(2)}) async-start(), calls=%async_computation.2 | async-start | bytes 2621440 | tf_op jit(solution)/shard_map/all_gather | solution.py:119
  11.2 15.0 %collective-permute-start.3 = (bf16[512,512]{1,0:T(8,128)(2,1)S(1)}, bf16[512,512]{1,0:T(8,128)(2,1)S(1)}, u32[]{:S(2)}, u32[]{:S(2)}) collective-permute-start(bf16[512,512]{1,0:T(8,128)(2,1)S(1)} %fusion.17), channel_id=1, source_target_pairs={{0,4},{4,0},{8,12},{12,8},{1,5},{5,1},{9,13},{13,9},{2,6},{6,2},{1... | collective-permute-start | bytes 1572872 | tf_op jit(solution)/shard_map/ppermute | solution.py:14
  26.2 25.3 %collective-permute-start.4 = (bf16[512,512]{1,0:T(8,128)(2,1)S(1)}, bf16[512,512]{1,0:T(8,128)(2,1)S(1)}, u32[]{:S(2)}, u32[]{:S(2)}) collective-permute-start(bf16[512,512]{1,0:T(8,128)(2,1)S(1)} %collective-permute-done.3), channel_id=1, source_target_pairs={{0,8},{8,0},{4,12},{12,4},{1,9},{9,1},{5,13},{13,5},{2,10},{10,2},... | collective-permute-start | bytes 1572872 | tf_op jit(solution)/shard_map/ppermute | solution.py:14
  56.7 5.6 %copy-start.12 = (s32[16]{0:T(128)S(1)}, s32[16]{0:T(128)}, u32[]{:S(2)}) copy-start(s32[16]{0:T(128)} %param.14) | copy-start | bytes 196
  56.7 175.0 %all-gather.7.cloned.1.call-start = ((), (), s32[]{:S(2)}) async-start(), calls=%async_computation.1 | async-start | bytes 10485760 | tf_op jit(solution)/shard_map/all_gather | solution.py:123
  57.4 353.6 %all-gather.11.cloned.1.call-start = ((), (), s32[]{:S(2)}) async-start(), calls=%async_computation.3 | async-start | bytes 2621440 | tf_op jit(solution)/shard_map/all_gather | solution.py:150
  59.7 172.0 %copy-start.13 = (f32[2048]{0:T(1024)S(1)}, f32[2048]{0:T(1024)}, u32[]{:S(2)}) copy-start(f32[2048]{0:T(1024)} %param.16) | copy-start | bytes 24580
  239.4 2.3 copy-start.3
  251.9 2.4 copy-start.2
  260.0 12.2 %collective-permute-start.5 = (bf16[128,512]{1,0:T(8,128)(2,1)}, bf16[128,512]{1,0:T(8,128)(2,1)}, u32[]{:S(2)}, u32[]{:S(2)}) collective-permute-start(bf16[128,512]{1,0:T(8,128)(2,1)} %slice_bitcast_fusion.2), channel_id=1, source_target_pairs={{0,4},{4,8},{8,12},{1,5},{5,9},{9,13},{2,6},{6,10},{10,14},{3,7},{... | collective-permute-start | bytes 393224 | tf_op jit(solution)/shard_map/ppermute | solution.py:20
  269.0 17.4 %collective-permute-start = (bf16[128,512]{1,0:T(8,128)(2,1)}, bf16[128,512]{1,0:T(8,128)(2,1)S(1)}, u32[]{:S(2)}, u32[]{:S(2)}) collective-permute-start(bf16[128,512]{1,0:T(8,128)(2,1)} %slice_bitcast_fusion.3), channel_id=1, source_target_pairs={{0,4},{4,8},{8,12},{1,5},{5,9},{9,13},{2,6},{6,10},{10,14},{3,7},{... | collective-permute-start | bytes 393224 | tf_op jit(solution)/shard_map/ppermute | solution.py:20
  277.3 9.1 %copy-start.10 = (bf16[512,512]{1,0:T(8,128)(2,1)S(1)}, bf16[512,512]{1,0:T(8,128)(2,1)}, u32[]{:S(2)}) copy-start(bf16[512,512]{1,0:T(8,128)(2,1)} %slice_bitcast_fusion.9) | copy-start | bytes 1572868
  282.2 0.8 copy-start.6
  283.6 9.9 %collective-permute-start.6 = (bf16[128,512]{1,0:T(8,128)(2,1)}, bf16[128,512]{1,0:T(8,128)(2,1)}, u32[]{:S(2)}, u32[]{:S(2)}) collective-permute-start(bf16[128,512]{1,0:T(8,128)(2,1)} %slice.178), channel_id=1, source_target_pairs={{0,4},{4,8},{8,12},{1,5},{5,9},{9,13},{2,6},{6,10},{10,14},{3,7},{... | collective-permute-start | bytes 393224 | tf_op jit(solution)/shard_map/ppermute | solution.py:20
  289.2 4.4 %copy-start.7 = (bf16[512,512]{1,0:T(8,128)(2,1)S(1)}, bf16[512,512]{1,0:T(8,128)(2,1)}, u32[]{:S(2)}) copy-start(bf16[512,512]{1,0:T(8,128)(2,1)} %copy-done.6) | copy-start | bytes 1572868
  302.9 5.1 %copy-start.9 = (bf16[4,128,256]{2,1,0:T(8,128)(2,1)S(1)}, bf16[4,128,256]{2,1,0:T(8,128)(2,1)}, u32[]{:S(2)}) copy-start(bf16[4,128,256]{2,1,0:T(8,128)(2,1)} %compare_convert_fusion) | copy-start | bytes 786436
  302.9 4.8 %collective-permute-start.7 = (bf16[128,512]{1,0:T(8,128)(2,1)S(1)}, bf16[128,512]{1,0:T(8,128)(2,1)S(1)}, u32[]{:S(2)}, u32[]{:S(2)}) collective-permute-start(bf16[128,512]{1,0:T(8,128)(2,1)S(1)} %slice.179), channel_id=1, source_target_pairs={{0,4},{4,8},{8,12},{1,5},{5,9},{9,13},{2,6},{6,10},{10,14},{3,7},{... | collective-permute-start | bytes 393224 | tf_op jit(solution)/shard_map/ppermute | solution.py:20
  305.7 2.2 copy-start.4
  305.8 10.8 %collective-permute-start.1 = (bf16[128,512]{1,0:T(8,128)(2,1)S(1)}, bf16[128,512]{1,0:T(8,128)(2,1)S(1)}, u32[]{:S(2)}, u32[]{:S(2)}) collective-permute-start(bf16[128,512]{1,0:T(8,128)(2,1)S(1)} %slice.169), channel_id=1, source_target_pairs={{0,4},{4,8},{8,12},{1,5},{5,9},{9,13},{2,6},{6,10},{10,14},{3,7},{... | collective-permute-start | bytes 393224 | tf_op jit(solution)/shard_map/ppermute | solution.py:20
  310.6 5.9 %copy-start.5 = (bf16[512,512]{1,0:T(8,128)(2,1)S(1)}, bf16[512,512]{1,0:T(8,128)(2,1)}, u32[]{:S(2)}) copy-start(bf16[512,512]{1,0:T(8,128)(2,1)} %copy-done.4) | copy-start | bytes 1572868
  312.3 4.5 %copy-start.8 = (bf16[4,128,256]{2,1,0:T(8,128)(2,1)S(1)}, bf16[4,128,256]{2,1,0:T(8,128)(2,1)}, u32[]{:S(2)}) copy-start(bf16[4,128,256]{2,1,0:T(8,128)(2,1)} %compare_convert_fusion.1) | copy-start | bytes 786436
  314.5 20.6 %collective-permute-start.8 = (bf16[512,512]{1,0:T(8,128)(2,1)}, bf16[512,512]{1,0:T(8,128)(2,1)}, u32[]{:S(2)}, u32[]{:S(2)}) collective-permute-start(bf16[512,512]{1,0:T(8,128)(2,1)} %fusion.21), channel_id=1, source_target_pairs={{0,4},{4,0},{8,12},{12,8},{1,5},{5,1},{9,13},{13,9},{2,6},{6,2},{1... | collective-permute-start | bytes 1572872 | tf_op jit(solution)/shard_map/ppermute | solution.py:14
  335.2 46.2 %collective-permute-start.9 = (bf16[512,512]{1,0:T(8,128)(2,1)}, bf16[512,512]{1,0:T(8,128)(2,1)S(1)}, u32[]{:S(2)}, u32[]{:S(2)}) collective-permute-start(bf16[512,512]{1,0:T(8,128)(2,1)} %collective-permute-done.8), channel_id=1, source_target_pairs={{0,8},{8,0},{4,12},{12,4},{1,9},{9,1},{5,13},{13,5},{2,10},{10,2},... | collective-permute-start | bytes 1572872 | tf_op jit(solution)/shard_map/ppermute | solution.py:14
  336.6 25.3 %collective-permute-start.2 = (bf16[128,512]{1,0:T(8,128)(2,1)S(1)}, bf16[128,512]{1,0:T(8,128)(2,1)S(1)}, u32[]{:S(2)}, u32[]{:S(2)}) collective-permute-start(bf16[128,512]{1,0:T(8,128)(2,1)S(1)} %slice.170), channel_id=1, source_target_pairs={{0,4},{4,8},{8,12},{1,5},{5,9},{9,13},{2,6},{6,10},{10,14},{3,7},{... | collective-permute-start | bytes 393224 | tf_op jit(solution)/shard_map/ppermute | solution.py:20
  383.5 8.7 %collective-permute-start.10 = (bf16[512,512]{1,0:T(8,128)(2,1)S(1)}, bf16[512,512]{1,0:T(8,128)(2,1)S(1)}, u32[]{:S(2)}, u32[]{:S(2)}) collective-permute-start(bf16[512,512]{1,0:T(8,128)(2,1)S(1)} %add_convert_fusion), channel_id=1, source_target_pairs={{0,1},{1,2},{2,3},{3,0},{4,5},{5,6},{6,7},{7,4},{8,9},{9,10},{10,1... | collective-permute-start | bytes 1572872 | tf_op jit(solution)/shard_map/ppermute | solution.py:88
  392.2 11.8 %collective-permute-start.11 = (bf16[512,512]{1,0:T(8,128)(2,1)S(1)}, bf16[512,512]{1,0:T(8,128)(2,1)S(1)}, u32[]{:S(2)}, u32[]{:S(2)}) collective-permute-start(bf16[512,512]{1,0:T(8,128)(2,1)S(1)} %collective-permute-done.10), channel_id=1, source_target_pairs={{0,1},{1,2},{2,3},{3,0},{4,5},{5,6},{6,7},{7,4},{8,9},{9,10},{10,1... | collective-permute-start | bytes 1572872 | tf_op jit(solution)/shard_map/ppermute | solution.py:88
  392.2 14.5 %collective-permute-start.12 = (bf16[512,512]{1,0:T(8,128)(2,1)S(1)}, bf16[512,512]{1,0:T(8,128)(2,1)S(1)}, u32[]{:S(2)}, u32[]{:S(2)}) collective-permute-start(bf16[512,512]{1,0:T(8,128)(2,1)S(1)} %add_convert_fusion), channel_id=1, source_target_pairs={{0,3},{1,0},{2,1},{3,2},{4,7},{5,4},{6,5},{7,6},{8,11},{9,8},{10,9... | collective-permute-start | bytes 1572872 | tf_op jit(solution)/shard_map/ppermute | solution.py:90
  409.2 6.0 %copy-start.1 = (bf16[4,512]{1,0:T(4,128)(2,1)S(1)}, bf16[4,512]{1,0:T(4,128)(2,1)}, u32[]{:S(2)}) copy-start(bf16[4,512]{1,0:T(4,128)(2,1)} %param.15) | copy-start | bytes 12292
Sparse Core Ops, SparseCore 0:
  9.6 25.2 all-gather.4
  56.8 23.5 all-gather.8
  82.0 149.6 all-gather.6
  316.3 67.1 all-gather.10
